TPU v7x, 32 devices: a whole 2x2x4 slice. The times are simulated.
32 devices in a mesh: dp: 8 (over z, y), hid: 4 (over x, core).
Axes of the slice: x: 2, y: 2, z: 4, core: 2. Of those that a mesh axis runs over, the one named last changes fastest.
Arguments:
- tokens: bfloat16 [16384, 1024], P('dp', 'hid'), may hold values from -6 to 6
- query_weight: bfloat16 [1024, 1024], P(None, 'hid'), may hold values from -0.1875 to 0.1875
- query_bias: float32 [1024], P('hid'), may hold values from -4 to 4
- key_weight: bfloat16 [1024, 1024], P(None, 'hid'), may hold values from -0.1875 to 0.1875
- value_weight: bfloat16 [1024, 1024], P(None, 'hid'), may hold values from -0.1875 to 0.1875
- value_bias: float32 [1024], P('hid'), may hold values from -4 to 4
- output_weight: bfloat16 [1024, 1024], P('hid'), may hold values from -0.75 to 0.75
- output_bias: float32 [1024], P('hid'), may hold values from -4 to 4
- attention_gain: float32 [1024], P('hid'), may hold values from 0.5 to 1.5
- attention_shift: float32 [1024], P('hid'), may hold values from -4 to 4
- inner_weight: bfloat16 [1024, 4096], P(None, 'hid'), may hold values from -0.1875 to 0.1875
- inner_bias: float32 [4096], P('hid'), may hold values from -4 to 4
- down_weight: bfloat16 [4096, 1024], P('hid'), may hold values from -0.1875 to 0.1875
- down_bias: float32 [1024], P('hid'), may hold values from -4 to 4
- final_gain: float32 [1024], P('hid'), may hold values from 0.5 to 1.5
- final_shift: float32 [1024], P('hid'), may hold values from -4 to 4
- head_alpha: float32 [16], replicated, may hold values from -1 to 3
- unit_alpha: float32 [4096], replicated, may hold values from -1 to 3
- width_alpha: float32 [1024], replicated, may hold values from -1 to 3
- multipliers: float32 [2], replicated, may hold values from -1 to 1
- head_noise: float32 [16], P('hid'), may hold values from 0.02 to 0.98
- unit_noise: float32 [4096], P('hid'), may hold values from 0.02 to 0.98
- width_noise: float32 [1024], P('hid'), may hold values from 0.02 to 0.98
- lengths: int32 [32], replicated, may hold values from 64 to 512, as said below
- teacher: bfloat16 [16384, 1024], P('dp', 'hid'), may hold values from -6 to 6
- upstream: bfloat16 [16384, 1024], P('dp', 'hid'), may hold values from -6 to 6
Outputs:
- output: bfloat16 [16384, 1024], P('dp', 'hid')
- tokens_grad: float32 [16384, 1024], P('dp', 'hid')
- query_weight_grad: float32 [1024, 1024], P(None, 'hid')
- query_bias_grad: float32 [1024], P('hid')
- key_weight_grad: float32 [1024, 1024], P(None, 'hid')
- value_weight_grad: float32 [1024, 1024], P(None, 'hid')
- value_bias_grad: float32 [1024], P('hid')
- output_weight_grad: float32 [1024, 1024], P('hid')
- output_bias_grad: float32 [1024], P('hid')
- attention_gain_grad: float32 [1024], P('hid')
- attention_shift_grad: float32 [1024], P('hid')
- inner_weight_grad: float32 [1024, 4096], P(None, 'hid')
- inner_bias_grad: float32 [4096], P('hid')
- down_weight_grad: float32 [4096, 1024], P('hid')
- down_bias_grad: float32 [1024], P('hid')
- final_gain_grad: float32 [1024], P('hid')
- final_shift_grad: float32 [1024], P('hid')
- head_alpha_grad: float32 [16], P('hid')
- unit_alpha_grad: float32 [4096], P('hid')
- width_alpha_grad: float32 [1024], P('hid')
- distill_mse: float32 [], replicated
- multipliers_new: float32 [2], replicated
Inputs may be any that keep to these rules, and one draw needn't show every extreme that they name: `lengths`: each sequence has 64 to 512 live tokens at its start; in every draw some sequence has 512 and some has 64.
All inputs are finite; a program needn't handle non-finite values.
Results may differ from a plain program's by a relative error of at most 0.02.
Values may be sent and summed in bfloat16 or wider, within the bound.
A program may use at most 192 MiB of HBM per device.

v0:
```python
import jax
import jax.numpy as jnp
from jax import lax
from jax.sharding import PartitionSpec as P

D = 1024
HD = 64
FF = 4096
SLOT = 512
BETA = 2.0 / 3.0
GAMMA = -0.1
ZETA = 1.1
TARGET = 0.7
ASCENT = 1.0
EPS = 1e-12
MASKED = -1000000000.0
ROOT_HALF = 0.7071067811865476
ROOT_TWO_PI = 2.5066282746310002


def erf_gelu(values):
    return 0.5 * values * (1.0 + lax.erf(values * ROOT_HALF))


def gelu_slope(values):
    return (
        0.5 * (1.0 + lax.erf(values * ROOT_HALF))
        + values * jnp.exp(-0.5 * values * values) / ROOT_TWO_PI
    )


def gate_value(noise, alpha):
    logits = (jnp.log(noise) - jnp.log(1.0 - noise) + alpha) / BETA
    stretched = jax.nn.sigmoid(logits) * (ZETA - GAMMA) + GAMMA
    return jnp.clip(stretched, 0.0, 1.0)


def keep_prob(alpha):
    return jax.nn.sigmoid(alpha - BETA * jnp.log(-GAMMA / ZETA))


def lagrangian(head_alpha, unit_alpha, width_alpha, multipliers):
    heads_kept = jnp.sum(keep_prob(head_alpha))
    units_kept = jnp.sum(keep_prob(unit_alpha))
    dims_kept = jnp.sum(keep_prob(width_alpha))
    full_size = 4.0 * D * D + 2.0 * D * FF
    expected = (4.0 * HD * heads_kept * dims_kept + 2.0 * units_kept * dims_kept) / full_size
    gap_value = 1.0 - expected - TARGET
    return multipliers[0] * gap_value + multipliers[1] * gap_value * gap_value


def inner_rows(left_side, right_side):
    return lax.dot_general(
        left_side, right_side, (((0,), (0,)), ((), ())), preferred_element_type=jnp.float32
    )


def times_transpose(left_side, right_side):
    return lax.dot_general(
        left_side, right_side, (((1,), (1,)), ((), ())), preferred_element_type=jnp.float32
    )


def gather_features(sharded):
    return lax.all_gather(sharded, "hid", axis=1, tiled=True)


def branch_total(partial_sum):
    return lax.psum_scatter(
        partial_sum.astype(jnp.bfloat16), "hid", scatter_dimension=1, tiled=True
    ).astype(jnp.float32)


def gather_grads(sharded):
    return lax.all_gather(sharded, "hid", axis=1, tiled=True)


def input_total(partial_sum):
    return lax.psum_scatter(
        partial_sum.astype(jnp.bfloat16), "hid", scatter_dimension=1, tiled=True
    ).astype(jnp.float32)


def norm_forward(residual, scale_gain, shift_bias):
    row_total = lax.psum(jnp.sum(residual, axis=1), "hid")
    row_mean = (row_total / D)[:, None]
    centered = residual - row_mean
    variance = (lax.psum(jnp.sum(centered * centered, axis=1), "hid") / D)[:, None]
    row_rstd = lax.rsqrt(variance + EPS)
    normed = (residual - row_mean) * row_rstd
    return (normed, row_rstd, normed * scale_gain + shift_bias)


def norm_backward(d_output, normed, row_rstd, scale_gain):
    d_normed = d_output * scale_gain
    sum_plain, sum_cross = lax.psum(
        (jnp.sum(d_normed, axis=1), jnp.sum(d_normed * normed, axis=1)), "hid"
    )
    return row_rstd * (d_normed - (sum_plain / D)[:, None] - normed * (sum_cross / D)[:, None])


def on_device(
    tokens,
    query_weight,
    query_bias,
    key_weight,
    value_weight,
    value_bias,
    output_weight,
    output_bias,
    attention_gain,
    attention_shift,
    inner_weight,
    inner_bias,
    down_weight,
    down_bias,
    final_gain,
    final_shift,
    head_alpha,
    unit_alpha,
    width_alpha,
    multipliers,
    head_noise,
    unit_noise,
    width_noise,
    lengths,
    teacher,
    upstream,
):
    row_count, local_width = tokens.shape
    heads_here = local_width // HD
    units_here = inner_weight.shape[1]
    seq_local = row_count // SLOT
    hid_rank = lax.axis_index("hid")
    data_rank = lax.axis_index("dp")
    scale_factor = HD ** (-0.5)
    local_lengths = lax.dynamic_slice_in_dim(lengths, data_rank * seq_local, seq_local)
    key_valid = jnp.arange(SLOT)[None, :] < local_lengths[:, None]
    live_rows = key_valid.reshape(row_count, 1).astype(jnp.float32)
    head_local = lax.dynamic_slice_in_dim(head_alpha, hid_rank * heads_here, heads_here)
    unit_local = lax.dynamic_slice_in_dim(unit_alpha, hid_rank * units_here, units_here)
    width_local = lax.dynamic_slice_in_dim(width_alpha, hid_rank * local_width, local_width)
    head_gate, head_pull = jax.vjp(
        lambda alpha_part: gate_value(head_noise, alpha_part), head_local
    )
    unit_gate, unit_pull = jax.vjp(
        lambda alpha_part: gate_value(unit_noise, alpha_part), unit_local
    )
    width_gate, width_pull = jax.vjp(
        lambda alpha_part: gate_value(width_noise, alpha_part), width_local
    )
    full_tokens = gather_features(tokens)
    shaped = (seq_local, SLOT, heads_here, HD)
    queries = (
        (jnp.dot(full_tokens, query_weight, preferred_element_type=jnp.float32) + query_bias)
        .astype(jnp.bfloat16)
        .reshape(shaped)
    )
    keys_all = (
        jnp.dot(full_tokens, key_weight, preferred_element_type=jnp.float32)
        .astype(jnp.bfloat16)
        .reshape(shaped)
    )
    values = (
        (jnp.dot(full_tokens, value_weight, preferred_element_type=jnp.float32) + value_bias)
        .astype(jnp.bfloat16)
        .reshape(shaped)
    )
    valid_keys = key_valid[:, None, None, :]

    def masked_scores():
        raw_scores = jnp.einsum(
            "sqhd,skhd->shqk", queries, keys_all, preferred_element_type=jnp.float32
        )
        return jnp.where(valid_keys, raw_scores * scale_factor, MASKED)

    scores = masked_scores()
    highest = jnp.max(scores, axis=-1, keepdims=True)
    exponent = jnp.exp(scores - highest)
    totals = jnp.sum(exponent, axis=-1, keepdims=True)
    log_total = highest + jnp.log(totals)
    context = jnp.einsum(
        "shqk,skhd->sqhd",
        (exponent / totals).astype(jnp.bfloat16),
        values,
        preferred_element_type=jnp.float32,
    ).reshape(row_count, heads_here, HD)
    gated_low = (
        (context * head_gate[None, :, None]).reshape(row_count, local_width).astype(jnp.bfloat16)
    )
    attention_pre = (
        branch_total(jnp.dot(gated_low, output_weight, preferred_element_type=jnp.float32))
        + output_bias
    )
    tokens_float = tokens.astype(jnp.float32)
    normed_one, rstd_one, middle = norm_forward(
        tokens_float + attention_pre * width_gate, attention_gain, attention_shift
    )
    middle_low = middle.astype(jnp.bfloat16)
    middle_full = gather_features(middle_low)
    pre_act = jnp.dot(middle_full, inner_weight, preferred_element_type=jnp.float32) + inner_bias
    activated = erf_gelu(pre_act)
    inner_act = (activated * unit_gate).astype(jnp.bfloat16)
    ffn_pre = (
        branch_total(jnp.dot(inner_act, down_weight, preferred_element_type=jnp.float32))
        + down_bias
    )
    normed_two, rstd_two, final_out = norm_forward(
        middle + ffn_pre * width_gate, final_gain, final_shift
    )
    differ = final_out - teacher.astype(jnp.float32)
    squared = lax.psum(jnp.sum(live_rows * differ * differ), ("dp", "hid"))
    distill_mse = squared / (jnp.sum(lengths).astype(jnp.float32) * D)
    d_final = live_rows * (upstream.astype(jnp.float32) + differ)
    final_gain_grad = jnp.sum(d_final * normed_two, axis=0)
    final_shift_grad = jnp.sum(d_final, axis=0)
    d_resid_two = norm_backward(d_final, normed_two, rstd_two, final_gain)
    width_grad = jnp.sum(d_resid_two * ffn_pre, axis=0)
    d_ffn_pre = d_resid_two * width_gate
    down_bias_grad = jnp.sum(d_ffn_pre, axis=0)
    d_ffn_full = gather_grads(d_ffn_pre.astype(jnp.bfloat16))
    down_weight_grad = inner_rows(inner_act, d_ffn_full)
    d_inner = times_transpose(d_ffn_full, down_weight)
    unit_grad = jnp.sum(d_inner * activated, axis=0)
    d_pre = (d_inner * unit_gate * gelu_slope(pre_act)).astype(jnp.bfloat16)
    inner_bias_grad = jnp.sum(d_pre.astype(jnp.float32), axis=0)
    inner_weight_grad = inner_rows(middle_full, d_pre)
    unit_alpha_task = unit_pull(unit_grad)[0]
    d_middle = d_resid_two + input_total(times_transpose(d_pre, inner_weight))
    attention_gain_grad = jnp.sum(d_middle * normed_one, axis=0)
    attention_shift_grad = jnp.sum(d_middle, axis=0)
    d_resid_one = norm_backward(d_middle, normed_one, rstd_one, attention_gain)
    width_grad = width_grad + jnp.sum(d_resid_one * attention_pre, axis=0)
    d_attn_pre = d_resid_one * width_gate
    output_bias_grad = jnp.sum(d_attn_pre, axis=0)
    d_attn_full = gather_grads(d_attn_pre.astype(jnp.bfloat16))
    output_weight_grad = inner_rows(gated_low, d_attn_full)
    d_gated = times_transpose(d_attn_full, output_weight).reshape(row_count, heads_here, HD)
    head_grad = jnp.sum(d_gated * context, axis=(0, 2))
    d_context = (d_gated * head_gate[None, :, None]).astype(jnp.bfloat16).reshape(shaped)
    d_probs = jnp.einsum("sqhd,skhd->shqk", d_context, values, preferred_element_type=jnp.float32)
    probabilities = jnp.exp(masked_scores() - log_total)
    d_scores = (
        probabilities * (d_probs - jnp.sum(probabilities * d_probs, axis=-1, keepdims=True))
    ).astype(jnp.bfloat16)
    d_queries = (
        (
            jnp.einsum("shqk,skhd->sqhd", d_scores, keys_all, preferred_element_type=jnp.float32)
            * scale_factor
        )
        .astype(jnp.bfloat16)
        .reshape(row_count, local_width)
    )
    d_keys = (
        (
            jnp.einsum("shqk,sqhd->skhd", d_scores, queries, preferred_element_type=jnp.float32)
            * scale_factor
        )
        .astype(jnp.bfloat16)
        .reshape(row_count, local_width)
    )
    d_values = (
        jnp.einsum(
            "shqk,sqhd->skhd",
            probabilities.astype(jnp.bfloat16),
            d_context,
            preferred_element_type=jnp.float32,
        )
        .astype(jnp.bfloat16)
        .reshape(row_count, local_width)
    )
    query_bias_grad = jnp.sum(d_queries.astype(jnp.float32), axis=0)
    value_bias_grad = jnp.sum(d_values.astype(jnp.float32), axis=0)
    query_weight_grad = inner_rows(full_tokens, d_queries)
    key_weight_grad = inner_rows(full_tokens, d_keys)
    value_weight_grad = inner_rows(full_tokens, d_values)
    d_tokens_part = (
        times_transpose(d_queries, query_weight)
        + times_transpose(d_keys, key_weight)
        + times_transpose(d_values, value_weight)
    )
    tokens_grad = d_resid_one + input_total(d_tokens_part)
    head_alpha_task = head_pull(head_grad)[0]
    width_alpha_task = width_pull(width_grad)[0]
    (
        query_weight_grad,
        query_bias_grad,
        key_weight_grad,
        value_weight_grad,
        value_bias_grad,
        output_weight_grad,
        output_bias_grad,
        attention_gain_grad,
        attention_shift_grad,
        inner_weight_grad,
        inner_bias_grad,
        down_weight_grad,
        down_bias_grad,
        final_gain_grad,
        final_shift_grad,
        head_alpha_task,
        unit_alpha_task,
        width_alpha_task,
    ) = (
        lax.psum(query_weight_grad.astype(jnp.bfloat16), "dp").astype(jnp.float32),
        lax.psum(query_bias_grad.astype(jnp.bfloat16), "dp").astype(jnp.float32),
        lax.psum(key_weight_grad.astype(jnp.bfloat16), "dp").astype(jnp.float32),
        lax.psum(value_weight_grad.astype(jnp.bfloat16), "dp").astype(jnp.float32),
        lax.psum(value_bias_grad.astype(jnp.bfloat16), "dp").astype(jnp.float32),
        lax.psum(output_weight_grad.astype(jnp.bfloat16), "dp").astype(jnp.float32),
        lax.psum(output_bias_grad.astype(jnp.bfloat16), "dp").astype(jnp.float32),
        lax.psum(attention_gain_grad.astype(jnp.bfloat16), "dp").astype(jnp.float32),
        lax.psum(attention_shift_grad.astype(jnp.bfloat16), "dp").astype(jnp.float32),
        lax.psum(inner_weight_grad.astype(jnp.bfloat16), "dp").astype(jnp.float32),
        lax.psum(inner_bias_grad.astype(jnp.bfloat16), "dp").astype(jnp.float32),
        lax.psum(down_weight_grad.astype(jnp.bfloat16), "dp").astype(jnp.float32),
        lax.psum(down_bias_grad.astype(jnp.bfloat16), "dp").astype(jnp.float32),
        lax.psum(final_gain_grad.astype(jnp.bfloat16), "dp").astype(jnp.float32),
        lax.psum(final_shift_grad.astype(jnp.bfloat16), "dp").astype(jnp.float32),
        lax.psum(head_alpha_task.astype(jnp.bfloat16), "dp").astype(jnp.float32),
        lax.psum(unit_alpha_task.astype(jnp.bfloat16), "dp").astype(jnp.float32),
        lax.psum(width_alpha_task.astype(jnp.bfloat16), "dp").astype(jnp.float32),
    )
    lag_grads = jax.grad(lagrangian, argnums=(0, 1, 2, 3))(
        head_alpha, unit_alpha, width_alpha, multipliers
    )
    head_alpha_grad = head_alpha_task + lax.dynamic_slice_in_dim(
        lag_grads[0], hid_rank * heads_here, heads_here
    )
    unit_alpha_grad = unit_alpha_task + lax.dynamic_slice_in_dim(
        lag_grads[1], hid_rank * units_here, units_here
    )
    width_alpha_grad = width_alpha_task + lax.dynamic_slice_in_dim(
        lag_grads[2], hid_rank * local_width, local_width
    )
    multipliers_new = multipliers + ASCENT * lag_grads[3]
    return (
        final_out.astype(jnp.bfloat16),
        tokens_grad,
        query_weight_grad,
        query_bias_grad,
        key_weight_grad,
        value_weight_grad,
        value_bias_grad,
        output_weight_grad,
        output_bias_grad,
        attention_gain_grad,
        attention_shift_grad,
        inner_weight_grad,
        inner_bias_grad,
        down_weight_grad,
        down_bias_grad,
        final_gain_grad,
        final_shift_grad,
        head_alpha_grad,
        unit_alpha_grad,
        width_alpha_grad,
        distill_mse,
        multipliers_new,
    )


def solution(mesh):
    return jax.shard_map(
        on_device,
        mesh=mesh,
        in_specs=(
            P("dp", "hid"),
            P(None, "hid"),
            P("hid"),
            P(None, "hid"),
            P(None, "hid"),
            P("hid"),
            P("hid", None),
            P("hid"),
            P("hid"),
            P("hid"),
            P(None, "hid"),
            P("hid"),
            P("hid", None),
            P("hid"),
            P("hid"),
            P("hid"),
            P(),
            P(),
            P(),
            P(),
            P("hid"),
            P("hid"),
            P("hid"),
            P(),
            P("dp", "hid"),
            P("dp", "hid"),
        ),
        out_specs=(
            P("dp", "hid"),
            P("dp", "hid"),
            P(None, "hid"),
            P("hid"),
            P(None, "hid"),
            P(None, "hid"),
            P("hid"),
            P("hid", None),
            P("hid"),
            P("hid"),
            P("hid"),
            P(None, "hid"),
            P("hid"),
            P("hid", None),
            P("hid"),
            P("hid"),
            P("hid"),
            P("hid"),
            P("hid"),
            P("hid"),
            P(),
            P(),
        ),
        check_vma=False,
    )
```

profile of v0, /device:TPU:0, one launch (start us, length us, event | category | flops | bytes accessed | tf_op | source)
XLA Modules:
  0.0 802.9 jit_solution(3298500553793230705)
XLA Ops:
  10.2 37.1 %all-gather.5.cloned.1.call-done = bf16[2048,1024]{1,0:T(8,128)(2,1)} async-done(((bf16[2048,256]{1,0:T(8,128)(2,1)}), bf16[2048,1024]{1,0:T(8,128)(2,1)}) %all-gather.5.cloned.1.call-update) | async-done | bytes 4194320 | tf_op jit(solution)/shard_map/all_gather | solution.py:65
  47.3 3.6 convolution_convert_fusion.3
  50.9 1.8 reshape.160
  52.7 4.0 copy.114
  56.7 3.6 fusion.13
  62.1 2.9 copy.113
  65.1 4.9 fusion.12
  70.0 4.4 reshape.158
  74.4 4.0 copy.115
  78.4 8.6 %fusion.60 = (f32[4,4,512]{2,1,0:T(4,128)S(1)}, f32[4,4,512,512]{2,3,1,0:T(8,128)}) fusion(bf16[4,512,4,64]{1,3,2,0:T(8,128)(2,1)S(1)} %copy.113, bf16[4,512,4,64]{1,3,2,0:T(8,128)(2,1)} %copy.114, pred[4,512]{1,0:T(4,128)(4,1)S(1)} %get-tuple-element.162), kind=kOutput, calls=%fused_computation.150 | convolution fusion | flops 549445632 | bytes 18909184 | tf_op jit(solution)/shard_map/sqhd,skhd->shqk/dot_general | solution.py:172
  87.0 8.3 %fusion = f32[4,4,512]{2,1,0:T(4,128)S(1)} fusion(f32[4,4,512,512]{2,3,1,0:T(8,128)} %get-tuple-element.165, f32[4,4,512]{2,1,0:T(4,128)S(1)} %get-tuple-element.164), kind=kLoop, calls=%fused_computation.6 | loop fusion | flops 8380416 | bytes 16842752 | tf_op jit(solution)/shard_map/reduce_sum | solution.py:180
  95.3 7.6 fusion.17
  106.5 3.4 convolution_convert_fusion
  111.9 42.6 %reduce-scatter.5.cloned.1.call-done = bf16[2048,256]{1,0:T(8,128)(2,1)} async-done(((bf16[2048,1024]{1,0:T(8,128)(2,1)}), bf16[2048,256]{1,0:T(8,128)(2,1)}) %reduce-scatter.5.cloned.1.call-update) | async-done | bytes 1048592 | tf_op jit(solution)/shard_map/reduce_scatter | solution.py:69
  156.3 5.9 psum.189
  162.1 2.0 multiply_reduce_fusion.10
  164.2 5.8 psum.190
  170.0 2.6 fusion.15
  172.7 35.8 %all-gather.7.cloned.1.call-done = bf16[2048,1024]{1,0:T(8,128)(2,1)} async-done(((bf16[2048,256]{1,0:T(8,128)(2,1)}), bf16[2048,1024]{1,0:T(8,128)(2,1)}) %all-gather.7.cloned.1.call-update) | async-done | bytes 4194320 | tf_op jit(solution)/shard_map/all_gather | solution.py:65
  208.5 9.6 %multiply_convert_fusion.1 = (bf16[2048,1024]{1,0:T(8,128)(2,1)S(1)}, f32[2048,1024]{1,0:T(8,128)}) fusion(f32[1024]{0:T(1024)S(1)} %fusion.37, f32[1024]{0:T(1024)S(1)} %copy-done.38, bf16[2048,1024]{1,0:T(8,128)(2,1)} %all-gather.7.cloned.1.call-done, bf16[1024,1024]{1,0:T(8,128)(2,1)} %param.36), kind=kOutput, calls=%fused_computation.19 | convolution fusion | flops 4309647360 | bytes 18882560 | tf_op jit(solution)/shard_map/dot_general | solution.py:201
  218.2 2.0 copy-done.50
  220.1 6.0 convolution_convert_fusion.2
  226.2 44.5 %reduce-scatter.7.cloned.1.call-done = bf16[2048,256]{1,0:T(8,128)(2,1)} async-done(((bf16[2048,1024]{1,0:T(8,128)(2,1)}), bf16[2048,256]{1,0:T(8,128)(2,1)}) %reduce-scatter.7.cloned.1.call-update) | async-done | bytes 1048592 | tf_op jit(solution)/shard_map/reduce_scatter | solution.py:69
  270.7 2.4 fusion.52
  273.2 5.9 psum.191
  279.1 2.7 multiply_reduce_fusion.9
  281.8 5.8 psum.192
  287.6 6.7 fusion.54
  294.3 10.6 %all-reduce.3 = (f32[2048]{0:T(1024)S(1)}, f32[2048]{0:T(1024)S(1)}) all-reduce(f32[2048]{0:T(1024)S(1)} %get-tuple-element.114, f32[2048]{0:T(1024)S(1)} %get-tuple-element.115), channel_id=1, replica_groups=mesh['dp'=8,'hid'=4] {'hid'}, use_global_device_ids=true, to_apply=%region_15.16 | all-reduce | flops 4096 | bytes 32768 | tf_op jit(solution)/shard_map/psum | solution.py:96
  304.9 5.9 multiply_convert_fusion.7
  310.9 35.9 %all-gather.9.cloned.1.call-done = bf16[2048,1024]{1,0:T(8,128)(2,1)} async-done(((bf16[2048,256]{1,0:T(8,128)(2,1)}), bf16[2048,1024]{1,0:T(8,128)(2,1)}) %all-gather.9.cloned.1.call-update) | async-done | bytes 4194320 | tf_op jit(solution)/shard_map/all_gather | solution.py:75
  346.8 12.4 %fusion.57 = (bf16[1024]{0:T(1024)(128)(2,1)S(1)}, bf16[2048,1024]{1,0:T(8,128)(2,1)S(1)}, f32[2048,1024]{1,0:T(8,128)}) fusion(f32[2048,1024]{1,0:T(8,128)} %get-tuple-element.167, f32[1024]{0:T(1024)S(1)} %copy-done.38, f32[1024]{0:T(1024)S(1)} %fusion.37, bf16[2048,1024]{1,0:T(8,128)(2,1)} %all-gather.9.cloned.1.call-done, ...), kind=kOutput, calls=%fused_computation.148 | convolution fusion | flops 4322229248 | bytes 27273216 | tf_op jit(solution)/shard_map/dot_general | solution.py:59
  359.2 2.0 copy-done.51
  361.2 6.3 convolution_convert_fusion.1
  367.6 44.5 %reduce-scatter.9.cloned.1.call-done = bf16[2048,256]{1,0:T(8,128)(2,1)} async-done(((bf16[2048,1024]{1,0:T(8,128)(2,1)}), bf16[2048,256]{1,0:T(8,128)(2,1)}) %reduce-scatter.9.cloned.1.call-update) | async-done | bytes 1048592 | tf_op jit(solution)/shard_map/reduce_scatter | solution.py:79
  412.1 3.4 multiply_reduce_fusion.6
  415.4 10.1 %all-reduce.2 = (f32[2048]{0:T(1024)S(1)}, f32[2048]{0:T(1024)S(1)}) all-reduce(f32[2048]{0:T(1024)S(1)} %get-tuple-element.111, f32[2048]{0:T(1024)S(1)} %get-tuple-element.117), channel_id=1, replica_groups=mesh['dp'=8,'hid'=4] {'hid'}, use_global_device_ids=true, to_apply=%region_20.21 | all-reduce | flops 4096 | bytes 32768 | tf_op jit(solution)/shard_map/psum | solution.py:96
  425.6 3.5 multiply_reduce_fusion.2
  432.4 2.0 copy.129
  434.4 9.5 %convolution_convert_fusion.4 = bf16[1024,1024]{1,0:T(8,128)(2,1)} fusion(bf16[2048,1024]{1,0:T(8,128)(2,1)} %copy-done.50, bf16[2048,1024]{1,0:T(8,128)(2,1)} %all-gather.9.cloned.1.call-done), kind=kOutput, calls=%fused_computation.64 | convolution fusion | flops 4296015872 | bytes 10485760 | tf_op jit(solution)/shard_map/dot_general | solution.py:53
  444.0 5.8 convolution_convert_fusion.5
  449.8 17.6 %all-gather.11.cloned.1.call-done = bf16[2048,1024]{1,0:T(8,128)(2,1)} async-done(((bf16[2048,256]{1,0:T(8,128)(2,1)}), bf16[2048,1024]{1,0:T(8,128)(2,1)}) %all-gather.11.cloned.1.call-update) | async-done | bytes 4194320 | tf_op jit(solution)/shard_map/all_gather | solution.py:75
  467.4 5.5 multiply_reduce_fusion.4
  472.9 5.1 reshape.157
  477.9 4.7 copy.119
  482.7 9.3 %fusion.62 = (bf16[4,64]{1,0:T(4,128)(2,1)S(1)}, bf16[4,512,4,64]{1,3,2,0:T(8,128)(2,1)S(1)}) fusion(f32[4,4,512,512]{2,3,1,0:T(8,128)} %get-tuple-element.165, f32[4,4,512]{2,1,0:T(4,128)S(1)} %bitcast.99, f32[4,512,4,64]{1,3,2,0:T(8,128)} %copy.119, f32[4]{0:T(128)S(1)} %get-tuple-element.155), kind=kOutput, calls=%fused_computation.152 | convolution fusion | flops 547356416 | bytes 19956240 | tf_op jit(solution)/shard_map/shqk,sqhd->skhd/dot_general | solution.py:263
  492.0 11.4 %multiply_reduce_fusion = (f32[4,4,512]{2,1,0:T(4,128)S(1)}, f32[4,4,512,512]{2,3,1,0:T(8,128)}) fusion(f32[4,4,512,512]{2,3,1,0:T(8,128)} %get-tuple-element.165, f32[4,4,512]{2,1,0:T(4,128)S(1)} %bitcast.100, bf16[4,512,4,64]{1,3,2,0:T(8,128)(2,1)S(1)} %copy-done.18, f32[4,512,4,64]{1,3,2,0:T(8,128)S(1)} %copy-done.7, f32[4]{0:T(128)S(1)} %get-tuple-element.155), kind=kOutput, calls=%fused_computation.1 | convolution fusion | flops 550494208 | bytes 36765712 | tf_op jit(solution)/shard_map/sqhd,skhd->shqk/dot_general | solution.py:241
  503.5 12.1 %multiply_convert_fusion = bf16[4,4,512,512]{2,3,1,0:T(8,128)(2,1)S(1)} fusion(f32[4,4,512,512]{2,3,1,0:T(8,128)} %get-tuple-element.170, f32[4,4,512,512]{2,3,1,0:T(8,128)} %get-tuple-element.165, f32[4,4,512]{2,1,0:T(4,128)S(1)} %get-tuple-element.169, f32[4,4,512]{2,1,0:T(4,128)S(1)} %bitcast.101), kind=kLoop, calls=%fused_computation | loop fusion | flops 16777216 | bytes 42008576 | tf_op jit(solution)/shard_map/convert_element_type | solution.py:245
  515.6 2.6 fusion.22
  524.2 2.1 convolution_convert_fusion.6
  526.9 2.0 fusion.29
  529.0 2.0 fusion.28
  531.0 2.1 fusion.27
  537.1 3.4 add_convert_fusion
  551.4 42.3 %psum.215 = f32[]{:T(128)} all-reduce(f32[]{:T(128)} %get-tuple-element.116), channel_id=1, replica_groups=mesh['dp'=8,'hid'=4] {'dp','hid'}, use_global_device_ids=true, to_apply=%region_59.60 | all-reduce | flops 1 | bytes 8 | tf_op jit(solution)/shard_map/psum | solution.py:212
  594.3 7.0 multiply_reduce_fusion.1
  601.8 23.1 %all-reduce.4 = (bf16[256]{0:T(256)(128)(2,1)S(1)}, bf16[256]{0:T(256)(128)(2,1)S(1)}, bf16[256]{0:T(256)(128)(2,1)S(1)}, bf16[256]{0:T(256)(128)(2,1)S(1)}, bf1...) all-reduce(bf16[256]{0:T(256)(128)(2,1)S(1)} %reduce_sum.283, ...), channel_id=1, replica_groups=mesh['dp'=8,'hid'=4] {'dp'}, use_global_device_ids=true, to_apply=%region_25.26 | all-reduce | flops 4356 | bytes 17424 | tf_op jit(solution)/shard_map/psum | solution.py:306
  631.9 113.6 %all-reduce.8.cloned.1.call-done = (bf16[1024,256]{0,1:T(8,128)(2,1)}, bf16[1024,256]{0,1:T(8,128)(2,1)}, bf16[1024,256]{0,1:T(8,128)(2,1)}, bf16[256,1024]{1,0:...) async-done(((bf16[1024,256]{0,1:T(8,128)(2,1)}, bf16[1024,256]{0,1:T(8,128)(2,1)}, bf16[1024,256]{0,1:T(8,128)(2,1)}, bf16[256,1024]{1,0:T(8,128)(2,1)}, ...) | async-done | bytes 6291472 | tf_op jit(solution)/shard_map/psum | solution.py:305
  745.5 2.3 copy.130
  747.8 2.4 copy.131
  752.4 2.8 convert_element_type.275
  755.3 2.5 convert_element_type.278
  757.7 33.6 %reduce-scatter.11.cloned.1.call-done = bf16[2048,256]{1,0:T(8,128)(2,1)} async-done(((bf16[2048,1024]{1,0:T(8,128)(2,1)}), bf16[2048,256]{1,0:T(8,128)(2,1)}) %reduce-scatter.11.cloned.1.call-update) | async-done | bytes 1048592 | tf_op jit(solution)/shard_map/reduce_scatter | solution.py:79
  791.4 3.4 convert_add_fusion
  (181 shorter events, 40.2 us)
Async XLA Ops:
  7.2 212.9 %copy-start = (bf16[1024,1024]{1,0:T(8,128)(2,1)S(1)}, bf16[1024,1024]{1,0:T(8,128)(2,1)}, u32[]{:S(2)}) copy-start(bf16[1024,1024]{1,0:T(8,128)(2,1)} %param.38) | copy-start | bytes 6291460
  7.2 40.1 %all-gather.5.cloned.1.call-start = ((), (), s32[]{:S(2)}) async-start(), calls=%async_computation.4 | async-start | bytes 5242880 | tf_op jit(solution)/shard_map/all_gather | solution.py:65
  7.9 146.6 %reduce-scatter.5.cloned.1.call-start = ((), (), s32[]{:S(2)}) async-start(), calls=%async_computation.5 | async-start | bytes 5242880 | tf_op jit(solution)/shard_map/reduce_scatter | solution.py:69
  52.7 4.1 copy-start.47
  62.1 2.9 copy-start.48
  65.1 13.4 %copy-start.9 = (bf16[4,512,4,64]{1,3,2,0:T(8,128)(2,1)}, bf16[4,512,4,64]{1,3,2,0:T(8,128)(2,1)S(1)}, u32[]{:S(2)}) copy-start(bf16[4,512,4,64]{1,3,2,0:T(8,128)(2,1)S(1)} %copy.113) | copy-start | bytes 3145732
  87.0 8.3 %copy-start.17 = (bf16[4,512,4,64]{1,3,2,0:T(8,128)(2,1)S(1)}, bf16[4,512,4,64]{1,3,2,0:T(8,128)(2,1)}, u32[]{:S(2)}) copy-start(bf16[4,512,4,64]{1,3,2,0:T(8,128)(2,1)} %copy.115) | copy-start | bytes 3145732
  104.2 2.3 copy-start.21
  105.1 1.4 copy-start.4
  109.9 0.7 copy-start.41
  109.9 44.6 %copy-start.2 = (bf16[2048,256]{1,0:T(8,128)(2,1)S(1)}, bf16[2048,256]{1,0:T(8,128)(2,1)}, u32[]{:S(2)}) copy-start(bf16[2048,256]{1,0:T(8,128)(2,1)} %param.26) | copy-start | bytes 3145732
  109.9 44.6 %copy-start.28 = (f32[256]{0:T(256)S(1)}, f32[256]{0:T(256)}, u32[]{:S(2)}) copy-start(f32[256]{0:T(256)} %param.33) | copy-start | bytes 3076
  109.9 98.6 %all-gather.7.cloned.1.call-start = ((), (), s32[]{:S(2)}) async-start(), calls=%async_computation.6 | async-start | bytes 5242880 | tf_op jit(solution)/shard_map/all_gather | solution.py:65
  154.5 15.4 %copy-start.30 = (f32[256]{0:T(256)S(1)}, f32[256]{0:T(256)}, u32[]{:S(2)}) copy-start(f32[256]{0:T(256)} %param.34) | copy-start | bytes 3076
  154.5 15.4 %copy-start.34 = (f32[256]{0:T(256)S(1)}, f32[256]{0:T(256)}, u32[]{:S(2)}) copy-start(f32[256]{0:T(256)} %param.35) | copy-start | bytes 3076
  170.0 2.7 copy-start.29
  170.0 2.7 copy-start.32
  170.0 38.5 %copy-start.38 = (f32[1024]{0:T(1024)S(1)}, f32[1024]{0:T(1024)}, u32[]{:S(2)}) copy-start(f32[1024]{0:T(1024)} %param.37) | copy-start | bytes 12292
  172.6 98.1 %reduce-scatter.7.cloned.1.call-start = ((), (), s32[]{:S(2)}) async-start(), calls=%async_computation.7 | async-start | bytes 5242880 | tf_op jit(solution)/shard_map/reduce_scatter | solution.py:69
  218.2 2.0 copy-start.50
  226.2 44.6 %copy-start.35 = (f32[256]{0:T(256)S(1)}, f32[256]{0:T(256)}, u32[]{:S(2)}) copy-start(f32[256]{0:T(256)} %param.39) | copy-start | bytes 3076
  226.2 120.6 %all-gather.9.cloned.1.call-start = ((), (), s32[]{:S(2)}) async-start(), calls=%async_computation.8 | async-start | bytes 5242880 | tf_op jit(solution)/shard_map/all_gather | solution.py:75
  273.2 14.4 %copy-start.39 = (f32[256]{0:T(256)S(1)}, f32[256]{0:T(256)}, u32[]{:S(2)}) copy-start(f32[256]{0:T(256)} %param.41) | copy-start | bytes 3076
  273.2 14.4 %copy-start.40 = (f32[256]{0:T(256)S(1)}, f32[256]{0:T(256)}, u32[]{:S(2)}) copy-start(f32[256]{0:T(256)} %param.40) | copy-start | bytes 3076
  310.8 101.2 %reduce-scatter.9.cloned.1.call-start = ((), (), s32[]{:S(2)}) async-start(), calls=%async_computation.9 | async-start | bytes 5242880 | tf_op jit(solution)/shard_map/reduce_scatter | solution.py:79
  346.8 14.4 %copy-start.46 = (bf16[1024,1024]{1,0:T(8,128)(2,1)S(1)}, bf16[1024,1024]{1,0:T(8,128)(2,1)}, u32[]{:S(2)}) copy-start(bf16[1024,1024]{1,0:T(8,128)(2,1)} %param.36) | copy-start | bytes 6291460
  359.2 2.0 copy-start.51
  367.5 44.6 %copy-start.3 = (bf16[2048,256]{1,0:T(8,128)(2,1)S(1)}, bf16[2048,256]{1,0:T(8,128)(2,1)}, u32[]{:S(2)}) copy-start(bf16[2048,256]{1,0:T(8,128)(2,1)} %reduce-scatter.5.cloned.1.call-done) | copy-start | bytes 3145732
  367.5 44.6 %copy-start.8 = (bf16[2048,256]{1,0:T(8,128)(2,1)S(1)}, bf16[2048,256]{1,0:T(8,128)(2,1)}, u32[]{:S(2)}) copy-start(bf16[2048,256]{1,0:T(8,128)(2,1)} %reduce-scatter.7.cloned.1.call-done) | copy-start | bytes 3145732
  367.5 99.9 %all-gather.11.cloned.1.call-start = ((), (), s32[]{:S(2)}) async-start(), calls=%async_computation.10 | async-start | bytes 5242880 | tf_op jit(solution)/shard_map/all_gather | solution.py:75
  429.1 1.3 copy-start.6
  430.5 2.0 copy-start.5
  431.7 313.8 %all-reduce.8.cloned.1.call-start = ((), (), s32[]{:S(2)}) async-start(), calls=%async_computation.12 | async-start | bytes 12582912 | tf_op jit(solution)/shard_map/psum | solution.py:305
  434.4 9.6 %copy-start.45 = (bf16[2048,1024]{1,0:T(8,128)(2,1)S(1)}, bf16[2048,1024]{1,0:T(8,128)(2,1)}, u32[]{:S(2)}) copy-start(bf16[2048,1024]{1,0:T(8,128)(2,1)} %all-gather.7.cloned.1.call-done) | copy-start | bytes 12582916
  434.4 9.6 %copy-start.52 = (bf16[2048,1024]{1,0:T(8,128)(2,1)S(1)}, bf16[2048,1024]{1,0:T(8,128)(2,1)}, u32[]{:S(2)}) copy-start(bf16[2048,1024]{1,0:T(8,128)(2,1)} %copy-done.51) | copy-start | bytes 12582916
  444.0 23.4 %copy-start.22 = (bf16[256,1024]{1,0:T(8,128)(2,1)S(1)}, bf16[256,1024]{1,0:T(8,128)(2,1)}, u32[]{:S(2)}) copy-start(bf16[256,1024]{1,0:T(8,128)(2,1)} %param.32) | copy-start | bytes 1572868
  482.7 9.3 %copy-start.7 = (f32[4,512,4,64]{1,3,2,0:T(8,128)S(1)}, f32[4,512,4,64]{1,3,2,0:T(8,128)}, u32[]{:S(2)}) copy-start(f32[4,512,4,64]{1,3,2,0:T(8,128)} %copy.119) | copy-start | bytes 6291460
  482.7 9.3 %copy-start.18 = (bf16[4,512,4,64]{1,3,2,0:T(8,128)(2,1)S(1)}, bf16[4,512,4,64]{1,3,2,0:T(8,128)(2,1)}, u32[]{:S(2)}) copy-start(bf16[4,512,4,64]{1,3,2,0:T(8,128)(2,1)} %copy.115) | copy-start | bytes 3145732
  503.5 12.1 %copy-start.10 = (bf16[4,512,4,64]{1,3,2,0:T(8,128)(2,1)S(1)}, bf16[4,512,4,64]{1,3,2,0:T(8,128)(2,1)}, u32[]{:S(2)}) copy-start(bf16[4,512,4,64]{1,3,2,0:T(8,128)(2,1)} %copy-done.9) | copy-start | bytes 3145732
  515.6 2.6 copy-start.11
  520.9 5.4 copy-start.15
  522.0 2.2 copy-start.12
  524.2 6.9 copy-start.13
  524.2 2.8 copy-start.44
  533.1 1.2 copy-start.14
  533.1 1.4 copy-start.23
  533.1 2.6 copy-start.24
  533.1 258.3 %reduce-scatter.11.cloned.1.call-start = ((), (), s32[]{:S(2)}) async-start(), calls=%async_computation.11 | async-start | bytes 5242880 | tf_op jit(solution)/shard_map/reduce_scatter | solution.py:79
  535.8 1.3 copy-start.16
  535.8 1.3 copy-start.25
  540.5 0.7 copy-start.49
  540.5 1.3 copy-start.36
  540.5 3.2 copy-start.42
  540.5 5.7 copy-start.31
  594.3 7.1 copy-start.33
  594.3 7.1 copy-start.37
  594.3 7.5 copy-start.43
  745.5 4.7 copy-start.27
  745.5 5.9 copy-start.26
  747.8 4.6 copy-start.20
  752.4 2.8 copy-start.19
  755.2 39.5 %copy-start.1 = (bf16[1024,1024]{1,0:T(8,128)(2,1)S(1)}, bf16[1024,1024]{1,0:T(8,128)(2,1)}, u32[]{:S(2)}) copy-start(bf16[1024,1024]{1,0:T(8,128)(2,1)} %param.38) | copy-start | bytes 6291460
Sparse Core Ops, SparseCore 0:
  9.6 37.7 all-gather.4
  110.0 44.4 reduce-scatter.4
  172.7 35.7 all-gather.6
  226.3 44.3 reduce-scatter.6
  311.0 35.7 all-gather.8
  367.6 44.3 reduce-scatter.8
  431.8 35.5 all-gather.10
  533.2 212.1 all-reduce.7
  748.0 43.3 reduce-scatter.10
where the time goes:
time: 813 us; the launch traced here: 803 us
  waiting for transfers between devices  406 us (50%)
  matrix products  126 us (15%)
  blocking collectives  109 us (13%)
  other arithmetic  82.2 us (10%)
  local copies, waits for them, and re-layouts  55.4 us (7%)
  between operations  23.3 us (3%)
    psum x1, waiting for transfers between devices, on_device(): lax.psum(query_weight_grad.astype(jnp.bfloat16), 'dp').astype(jnp.float32)  114 us
    reduce_scatter x2, waiting for transfers between devices, branch_total(): lax.psum_scatter(partial_sum.astype(jnp.bfloat16), 'hid', scatter_dimensi...  87.1 us
    reduce_scatter x2, waiting for transfers between devices, input_total(): lax.psum_scatter(partial_sum.astype(jnp.bfloat16), 'hid', scatter_dimensi...  78.2 us
    all_gather x2, waiting for transfers between devices, gather_features(): return lax.all_gather(sharded, 'hid', axis=1, tiled=True)  72.9 us
    all_gather x2, waiting for transfers between devices, gather_grads(): return lax.all_gather(sharded, 'hid', axis=1, tiled=True)  53.5 us
    psum x1, blocking collectives, on_device(): squared = lax.psum(jnp.sum(live_rows * differ * differ), ('dp', 'hid'))  42.3 us
    dot_general x6, matrix products, times_transpose(): lax.dot_general(left_side, right_side, (((1,), (1,)), ((), ())), preferre...  30.1 us
    dot_general x6, matrix products, inner_rows(): lax.dot_general(left_side, right_side, (((0,), (0,)), ((), ())), preferre...  23.6 us
  transfers between devices with their start and end apart: 9, of which 9 were waited for; matrix products, arithmetic and copies ran while one was open for 7% of the time, Pallas kernels for 0%

commit v1 on v0

--- a/solution.py
+++ b/solution.py
@@ -1,3 +1,4 @@
+import functools
 import jax
 import jax.numpy as jnp
 from jax import lax
@@ -18,6 +19,39 @@
 ROOT_TWO_PI = 2.5066282746310002
 
 
+def treat_the_bands(x_local, array_axis):
+    oldest, vec_out, piece_now = (
+        lax.axis_size("hid"),
+        lax.axis_index("hid"),
+        x_local.shape[array_axis],
+    )
+    store = list(map(lambda u: (u, (u + 1) % oldest), range(oldest)))
+    inbox = list(map(lambda u: (u, (u - 1) % oldest), range(oldest)))
+    z_new = jnp.zeros(
+        (*x_local.shape[:array_axis], oldest * piece_now, *x_local.shape[array_axis + 1 :]),
+        x_local.dtype,
+    )
+    outer = front = x_local
+    met_up = oldest // 2
+    hop_no = 1
+    z_new = lax.dynamic_update_slice_in_dim(z_new, x_local, vec_out * piece_now, axis=array_axis)
+    while hop_no < met_up + 1:
+        outer = lax.ppermute(outer, "hid", store)
+        z_new = lax.dynamic_update_slice_in_dim(
+            z_new, outer, (vec_out - hop_no) % oldest * piece_now, axis=array_axis
+        )
+        if hop_no < oldest - met_up:
+            front = lax.ppermute(front, "hid", inbox)
+            z_new = lax.dynamic_update_slice_in_dim(
+                z_new, front, (vec_out + hop_no) % oldest * piece_now, axis=array_axis
+            )
+        hop_no = hop_no + 1
+    return z_new
+
+
+_start_shapes = functools.partial(treat_the_bands, array_axis=1)
+
+
 def erf_gelu(values):
     return 0.5 * values * (1.0 + lax.erf(values * ROOT_HALF))
 
@@ -62,7 +96,7 @@
 
 
 def gather_features(sharded):
-    return lax.all_gather(sharded, "hid", axis=1, tiled=True)
+    return _start_shapes(sharded)
 
 
 def branch_total(partial_sum):

time: 813 us -> 827 us (1.017)
  local copies, waits for them, and re-layouts: 55.4 us -> 73.7 us
  waiting for transfers between devices: 406 us -> 396 us
    all_gather x2 -> x0, waiting for transfers between devices: 72.9 us -> none  [gather_features(): return lax.all_gather(sharded, 'hid', axis=1, tiled=True)]
    ppermute x0 -> x6, waiting for transfers between devices: none -> 57.7 us  [the longest x4 57.7 us: treat_the_bands(): outer = lax.ppermute(outer, 'hid', store)]
    dynamic_update_slice x0 -> x7, local copies, waits for them, and re-layouts: none -> 11.2 us  [the longest x4 7.26 us: treat_the_bands(): lax.dynamic_update_slice_in_dim(z_new, outer, (vec_out - hop_no) % oldest...]
    unnamed x114 -> x123, local copies, waits for them, and re-layouts: 19 us -> 18.4 us
  transfers between devices with their start and end apart: 9 -> 13, of which waited for: 9 -> 11; matrix products, arithmetic and copies ran while one was open for 7% -> 8% of each run, Pallas kernels for 0% -> 0%
where the time goes in v1:
time: 827 us; the launch traced here: 823 us
  waiting for transfers between devices  396 us (48%)
  matrix products  125 us (15%)
  blocking collectives  109 us (13%)
  other arithmetic  86.7 us (10%)
  local copies, waits for them, and re-layouts  73.7 us (9%)
  between operations  23.4 us (3%)
  starting transfers between devices  8.47 us (1%)
    psum x1, waiting for transfers between devices, on_device(): lax.psum(query_weight_grad.astype(jnp.bfloat16), 'dp').astype(jnp.float32)  114 us
    reduce_scatter x2, waiting for transfers between devices, branch_total(): lax.psum_scatter(partial_sum.astype(jnp.bfloat16), 'hid', scatter_dimensi...  92.2 us
    reduce_scatter x2, waiting for transfers between devices, input_total(): lax.psum_scatter(partial_sum.astype(jnp.bfloat16), 'hid', scatter_dimensi...  78.7 us
    ppermute x4, waiting for transfers between devices, treat_the_bands(): outer = lax.ppermute(outer, 'hid', store)  57.7 us
    all_gather x2, waiting for transfers between devices, gather_grads(): return lax.all_gather(sharded, 'hid', axis=1, tiled=True)  53.7 us
    psum x1, blocking collectives, on_device(): squared = lax.psum(jnp.sum(live_rows * differ * differ), ('dp', 'hid'))  42.3 us
    dot_general x6, matrix products, times_transpose(): lax.dot_general(left_side, right_side, (((1,), (1,)), ((), ())), preferre...  30.2 us
    dot_general x6, matrix products, inner_rows(): lax.dot_general(left_side, right_side, (((0,), (0,)), ((), ())), preferre...  23.9 us
  transfers between devices with their start and end apart: 13, of which 11 were waited for; matrix products, arithmetic and copies ran while one was open for 8% of the time, Pallas kernels for 0%

profile of v1, /device:TPU:0, one launch (start us, length us, event | category | flops | bytes accessed | tf_op | source)
XLA Modules:
  0.0 822.8 jit_solution(14571504317886829301)
XLA Ops:
  9.8 21.4 %collective-permute-done = bf16[2048,256]{1,0:T(8,128)(2,1)} collective-permute-done((bf16[2048,256]{1,0:T(8,128)(2,1)}, bf16[2048,256]{1,0:T(8,128)(2,1)}, u32[]{:S(2)}, u32[]{:S(2)}) %collective-permute-start) | collective-permute-done | bytes 1048608 | tf_op jit(solution)/shard_map/ppermute | solution.py:39
  31.2 2.4 collective-permute-start.2
  40.0 5.7 collective-permute-done.2
  49.1 2.2 convolution_convert_fusion.3
  51.3 4.9 reshape.160
  56.2 4.0 copy.105
  60.3 4.5 fusion.13
  64.8 4.4 reshape.159
  69.2 4.0 copy.104
  73.3 4.5 fusion.12
  77.8 4.4 reshape.158
  82.2 4.0 copy.106
  86.3 9.0 %fusion.58 = (f32[4,4,512]{2,1,0:T(4,128)S(1)}, f32[4,4,512,512]{2,3,1,0:T(8,128)}) fusion(bf16[4,512,4,64]{1,3,2,0:T(8,128)(2,1)} %copy.104, bf16[4,512,4,64]{1,3,2,0:T(8,128)(2,1)} %copy.105, pred[4,512]{1,0:T(4,128)(4,1)S(1)} %get-tuple-element.76), kind=kOutput, calls=%fused_computation.155 | convolution fusion | flops 549445632 | bytes 18909184 | tf_op jit(solution)/shard_map/sqhd,skhd->shqk/dot_general | solution.py:206
  95.2 8.3 %fusion = f32[4,4,512]{2,1,0:T(4,128)S(1)} fusion(f32[4,4,512,512]{2,3,1,0:T(8,128)} %get-tuple-element.79, f32[4,4,512]{2,1,0:T(4,128)S(1)} %get-tuple-element.78), kind=kLoop, calls=%fused_computation.6 | loop fusion | flops 8380416 | bytes 16842752 | tf_op jit(solution)/shard_map/reduce_sum | solution.py:214
  103.5 7.5 fusion.17
  114.6 3.4 convolution_convert_fusion
  120.0 46.4 %reduce-scatter.5.cloned.1.call-done = bf16[2048,256]{1,0:T(8,128)(2,1)} async-done(((bf16[2048,1024]{1,0:T(8,128)(2,1)}), bf16[2048,256]{1,0:T(8,128)(2,1)}) %reduce-scatter.5.cloned.1.call-update) | async-done | bytes 1048592 | tf_op jit(solution)/shard_map/reduce_scatter | solution.py:103
  168.1 5.9 psum.189
  176.0 5.8 psum.190
  188.3 22.1 %collective-permute-done.3 = bf16[2048,256]{1,0:T(8,128)(2,1)} collective-permute-done((bf16[2048,256]{1,0:T(8,128)(2,1)}, bf16[2048,256]{1,0:T(8,128)(2,1)}, u32[]{:S(2)}, u32[]{:S(2)}) %collective-permute-start.3) | collective-permute-done | bytes 1048608 | tf_op jit(solution)/shard_map/ppermute | solution.py:39
  211.7 2.3 constant_dynamic-update-slice_fusion.2
  214.0 2.4 constant_dynamic-update-slice_fusion.1
  216.4 8.6 %collective-permute-done.5 = bf16[2048,256]{1,0:T(8,128)(2,1)} collective-permute-done((bf16[2048,256]{1,0:T(8,128)(2,1)}, bf16[2048,256]{1,0:T(8,128)(2,1)}, u32[]{:S(2)}, u32[]{:S(2)}) %collective-permute-start.5) | collective-permute-done | bytes 1048608 | tf_op jit(solution)/shard_map/ppermute | solution.py:39
  225.0 2.3 constant_dynamic-update-slice_fusion
  227.2 9.1 %multiply_convert_fusion.1 = (bf16[2048,1024]{1,0:T(8,128)(2,1)S(1)}, f32[2048,1024]{1,0:T(8,128)}) fusion(f32[1024]{0:T(1024)S(1)} %fusion.34, f32[1024]{0:T(1024)S(1)} %copy-done.44, bf16[2048,1024]{1,0:T(8,128)(2,1)} %constant_dynamic-update-slice_fusion, bf16[1024,1024]{1,0:T(8,128)(2,1)S(1)} %copy-done.51), kind=kOutput, calls=%fused_computation.19 | convolution fusion | flops 4309647360 | bytes 18882560 | tf_op jit(solution)/shard_map/dot_general | solution.py:235
  238.2 6.0 convolution_convert_fusion.2
  244.6 45.8 %reduce-scatter.7.cloned.1.call-done = bf16[2048,256]{1,0:T(8,128)(2,1)} async-done(((bf16[2048,1024]{1,0:T(8,128)(2,1)}), bf16[2048,256]{1,0:T(8,128)(2,1)}) %reduce-scatter.7.cloned.1.call-update) | async-done | bytes 1048592 | tf_op jit(solution)/shard_map/reduce_scatter | solution.py:103
  290.4 2.4 fusion.49
  292.8 5.9 psum.191
  298.7 2.7 multiply_reduce_fusion.9
  301.4 5.8 psum.192
  307.2 6.3 fusion.51
  313.5 10.6 %all-reduce.3 = (f32[2048]{0:T(1024)S(1)}, f32[2048]{0:T(1024)S(1)}) all-reduce(f32[2048]{0:T(1024)S(1)} %get-tuple-element.26, f32[2048]{0:T(1024)S(1)} %get-tuple-element.27), channel_id=1, replica_groups=mesh['dp'=8,'hid'=4] {'hid'}, use_global_device_ids=true, to_apply=%region_15.16 | all-reduce | flops 4096 | bytes 32768 | tf_op jit(solution)/shard_map/psum | solution.py:130
  324.1 5.9 multiply_convert_fusion.7
  330.1 35.9 %all-gather.3.cloned.1.call-done = bf16[2048,1024]{1,0:T(8,128)(2,1)} async-done(((bf16[2048,256]{1,0:T(8,128)(2,1)}), bf16[2048,1024]{1,0:T(8,128)(2,1)}) %all-gather.3.cloned.1.call-update) | async-done | bytes 4194320 | tf_op jit(solution)/shard_map/all_gather | solution.py:109
  366.0 12.4 %fusion.54 = (bf16[1024]{0:T(1024)(128)(2,1)S(1)}, bf16[2048,1024]{1,0:T(8,128)(2,1)S(1)}, f32[2048,1024]{1,0:T(8,128)}) fusion(f32[2048,1024]{1,0:T(8,128)} %get-tuple-element.81, f32[1024]{0:T(1024)S(1)} %copy-done.44, f32[1024]{0:T(1024)S(1)} %fusion.34, bf16[2048,1024]{1,0:T(8,128)(2,1)} %all-gather.3.cloned.1.call-done, bf16[1024,1024]{1,0:T(8,128)(2,1)S(1)} %copy-done), kind=kOutput, calls=%fused_computation.153 | convolution fusion | flops 4322229248 | bytes 27273216 | tf_op jit(solution)/shard_map/dot_general | solution.py:93
  380.4 6.3 convolution_convert_fusion.1
  386.8 44.5 %reduce-scatter.9.cloned.1.call-done = bf16[2048,256]{1,0:T(8,128)(2,1)} async-done(((bf16[2048,1024]{1,0:T(8,128)(2,1)}), bf16[2048,256]{1,0:T(8,128)(2,1)}) %reduce-scatter.9.cloned.1.call-update) | async-done | bytes 1048592 | tf_op jit(solution)/shard_map/reduce_scatter | solution.py:113
  431.3 3.4 multiply_reduce_fusion.6
  434.7 10.1 %all-reduce.2 = (f32[2048]{0:T(1024)S(1)}, f32[2048]{0:T(1024)S(1)}) all-reduce(f32[2048]{0:T(1024)S(1)} %get-tuple-element.23, f32[2048]{0:T(1024)S(1)} %get-tuple-element.29), channel_id=1, replica_groups=mesh['dp'=8,'hid'=4] {'hid'}, use_global_device_ids=true, to_apply=%region_20.21 | all-reduce | flops 4096 | bytes 32768 | tf_op jit(solution)/shard_map/psum | solution.py:130
  444.8 3.5 multiply_reduce_fusion.2
  453.5 9.5 %convolution_convert_fusion.5 = bf16[1024,1024]{1,0:T(8,128)(2,1)} fusion(bf16[2048,1024]{1,0:T(8,128)(2,1)} %constant_dynamic-update-slice_fusion, bf16[2048,1024]{1,0:T(8,128)(2,1)} %copy-done.58), kind=kOutput, calls=%fused_computation.65 | convolution fusion | flops 4296015872 | bytes 10485760 | tf_op jit(solution)/shard_map/dot_general | solution.py:87
  463.0 5.8 convolution_convert_fusion.4
  468.9 17.8 %all-gather.5.cloned.1.call-done = bf16[2048,1024]{1,0:T(8,128)(2,1)} async-done(((bf16[2048,256]{1,0:T(8,128)(2,1)}), bf16[2048,1024]{1,0:T(8,128)(2,1)}) %all-gather.5.cloned.1.call-update) | async-done | bytes 4194320 | tf_op jit(solution)/shard_map/all_gather | solution.py:109
  486.7 5.5 multiply_reduce_fusion.4
  492.2 5.1 reshape.157
  497.2 4.8 copy.110
  502.0 9.3 %fusion.60 = (bf16[4,64]{1,0:T(4,128)(2,1)S(1)}, bf16[4,512,4,64]{1,3,2,0:T(8,128)(2,1)S(1)}) fusion(f32[4,4,512,512]{2,3,1,0:T(8,128)} %get-tuple-element.79, f32[4,4,512]{2,1,0:T(4,128)S(1)} %bitcast.93, f32[4,512,4,64]{1,3,2,0:T(8,128)} %copy.110, f32[4]{0:T(128)S(1)} %copy-done.41), kind=kOutput, calls=%fused_computation.157 | convolution fusion | flops 547356416 | bytes 19956240 | tf_op jit(solution)/shard_map/shqk,sqhd->skhd/dot_general | solution.py:297
  511.4 11.4 %multiply_reduce_fusion = (f32[4,4,512]{2,1,0:T(4,128)S(1)}, f32[4,4,512,512]{2,3,1,0:T(8,128)}) fusion(f32[4,4,512,512]{2,3,1,0:T(8,128)} %get-tuple-element.79, f32[4,4,512]{2,1,0:T(4,128)S(1)} %bitcast.94, bf16[4,512,4,64]{1,3,2,0:T(8,128)(2,1)S(1)} %copy-done.21, f32[4,512,4,64]{1,3,2,0:T(8,128)S(1)} %copy-done.8, f32[4]{0:T(128)S(1)} %copy-done.41), kind=kOutput, calls=%fused_computation.1 | convolution fusion | flops 550494208 | bytes 36765712 | tf_op jit(solution)/shard_map/sqhd,skhd->shqk/dot_general | solution.py:275
  522.7 12.1 %multiply_convert_fusion = bf16[4,4,512,512]{2,3,1,0:T(8,128)(2,1)S(1)} fusion(f32[4,4,512,512]{2,3,1,0:T(8,128)} %get-tuple-element.84, f32[4,4,512,512]{2,3,1,0:T(8,128)} %get-tuple-element.79, f32[4,4,512]{2,1,0:T(4,128)S(1)} %get-tuple-element.83, f32[4,4,512]{2,1,0:T(4,128)S(1)} %bitcast.95), kind=kLoop, calls=%fused_computation | loop fusion | flops 16777216 | bytes 42008576 | tf_op jit(solution)/shard_map/convert_element_type | solution.py:279
  534.9 2.6 fusion.22
  548.1 2.1 convolution_convert_fusion.9
  550.8 2.1 convolution_convert_fusion.6
  557.0 3.4 add_convert_fusion
  571.2 42.3 %psum.215 = f32[]{:T(128)} all-reduce(f32[]{:T(128)} %get-tuple-element.28), channel_id=1, replica_groups=mesh['dp'=8,'hid'=4] {'dp','hid'}, use_global_device_ids=true, to_apply=%region_59.60 | all-reduce | flops 1 | bytes 8 | tf_op jit(solution)/shard_map/psum | solution.py:246
  614.2 7.0 multiply_reduce_fusion.1
  621.7 23.1 %all-reduce.4 = (bf16[256]{0:T(256)(128)(2,1)S(1)}, bf16[256]{0:T(256)(128)(2,1)S(1)}, bf16[256]{0:T(256)(128)(2,1)S(1)}, bf16[256]{0:T(256)(128)(2,1)S(1)}, bf1...) all-reduce(bf16[256]{0:T(256)(128)(2,1)S(1)} %reduce_sum.283, ...), channel_id=1, replica_groups=mesh['dp'=8,'hid'=4] {'dp'}, use_global_device_ids=true, to_apply=%region_25.26 | all-reduce | flops 4356 | bytes 17424 | tf_op jit(solution)/shard_map/psum | solution.py:340
  651.8 113.6 %all-reduce.8.cloned.1.call-done = (bf16[1024,256]{1,0:T(8,128)(2,1)}, bf16[1024,256]{1,0:T(8,128)(2,1)}, bf16[1024,256]{1,0:T(8,128)(2,1)}, bf16[256,1024]{1,0:...) async-done(((bf16[1024,256]{1,0:T(8,128)(2,1)}, bf16[1024,256]{1,0:T(8,128)(2,1)}, bf16[1024,256]{1,0:T(8,128)(2,1)}, bf16[256,1024]{1,0:T(8,128)(2,1)}, ...) | async-done | bytes 6291472 | tf_op jit(solution)/shard_map/psum | solution.py:339
  765.3 2.2 convert_element_type.247
  767.5 2.2 convert_element_type.250
  771.9 2.6 convert_element_type.263
  774.5 2.6 convert_element_type.266
  777.1 34.2 %reduce-scatter.11.cloned.1.call-done = bf16[2048,256]{1,0:T(8,128)(2,1)} async-done(((bf16[2048,1024]{1,0:T(8,128)(2,1)}), bf16[2048,256]{1,0:T(8,128)(2,1)}) %reduce-scatter.11.cloned.1.call-update) | async-done | bytes 1048592 | tf_op jit(solution)/shard_map/reduce_scatter | solution.py:113
  811.2 3.4 convert_add_fusion
  (208 shorter events, 67.8 us)
Async XLA Ops:
  7.2 231.0 %copy-start = (bf16[1024,1024]{1,0:T(8,128)(2,1)S(1)}, bf16[1024,1024]{1,0:T(8,128)(2,1)}, u32[]{:S(2)}) copy-start(bf16[1024,1024]{1,0:T(8,128)(2,1)} %param.38) | copy-start | bytes 6291460
  7.2 159.2 %reduce-scatter.5.cloned.1.call-start = ((), (), s32[]{:S(2)}) async-start(), calls=%async_computation.4 | async-start | bytes 5242880 | tf_op jit(solution)/shard_map/reduce_scatter | solution.py:103
  7.3 23.9 %collective-permute-start = (bf16[2048,256]{1,0:T(8,128)(2,1)}, bf16[2048,256]{1,0:T(8,128)(2,1)}, u32[]{:S(2)}, u32[]{:S(2)}) collective-permute-start(bf16[2048,256]{1,0:T(8,128)(2,1)} %param.26), channel_id=1, source_target_pairs={{0,1},{1,2},{2,3},{3,0},{4,5},{5,6},{6,7},{7,4},{8,9},{9,10},{10,1... | collective-permute-start | bytes 3145736 | tf_op jit(solution)/shard_map/ppermute | solution.py:39
  7.8 30.8 %collective-permute-start.1 = (bf16[2048,256]{1,0:T(8,128)(2,1)}, bf16[2048,256]{1,0:T(8,128)(2,1)}, u32[]{:S(2)}, u32[]{:S(2)}) collective-permute-start(bf16[2048,256]{1,0:T(8,128)(2,1)} %param.26), channel_id=1, source_target_pairs={{0,3},{1,0},{2,1},{3,2},{4,7},{5,4},{6,5},{7,6},{8,11},{9,8},{10,9... | collective-permute-start | bytes 3145736 | tf_op jit(solution)/shard_map/ppermute | solution.py:44
  31.2 14.5 %collective-permute-start.2 = (bf16[2048,256]{1,0:T(8,128)(2,1)}, bf16[2048,256]{1,0:T(8,128)(2,1)}, u32[]{:S(2)}, u32[]{:S(2)}) collective-permute-start(bf16[2048,256]{1,0:T(8,128)(2,1)} %collective-permute-done), channel_id=1, source_target_pairs={{0,1},{1,2},{2,3},{3,0},{4,5},{5,6},{6,7},{7,4},{8,9},{9,10},{10,1... | collective-permute-start | bytes 3145736 | tf_op jit(solution)/shard_map/ppermute | solution.py:39
  38.6 10.5 %copy-start.27 = (bf16[1024,256]{1,0:T(8,128)(2,1)S(1)}, bf16[1024,256]{1,0:T(8,128)(2,1)}, u32[]{:S(2)}) copy-start(bf16[1024,256]{1,0:T(8,128)(2,1)} %param.29) | copy-start | bytes 1572868
  47.1 2.0 copy-start.18
  56.2 4.1 copy-start.53
  69.2 4.1 copy-start.54
  95.2 8.3 %copy-start.20 = (bf16[4,512,4,64]{1,3,2,0:T(8,128)(2,1)S(1)}, bf16[4,512,4,64]{1,3,2,0:T(8,128)(2,1)}, u32[]{:S(2)}) copy-start(bf16[4,512,4,64]{1,3,2,0:T(8,128)(2,1)} %copy.106) | copy-start | bytes 3145732
  112.4 2.2 copy-start.24
  113.3 1.3 copy-start.5
  118.0 48.4 %copy-start.32 = (f32[256]{0:T(256)S(1)}, f32[256]{0:T(256)}, u32[]{:S(2)}) copy-start(f32[256]{0:T(256)} %param.33) | copy-start | bytes 3076
  118.0 172.3 %reduce-scatter.7.cloned.1.call-start = ((), (), s32[]{:S(2)}) async-start(), calls=%async_computation.5 | async-start | bytes 5242880 | tf_op jit(solution)/shard_map/reduce_scatter | solution.py:103
  183.0 27.9 %copy-start.36 = (f32[1024]{0:T(1024)S(1)}, f32[1024]{0:T(1024)}, u32[]{:S(2)}) copy-start(f32[1024]{0:T(1024)} %param.47) | copy-start | bytes 12292
  184.6 2.0 copy-start.17
  186.6 23.8 %collective-permute-start.3 = (bf16[2048,256]{1,0:T(8,128)(2,1)}, bf16[2048,256]{1,0:T(8,128)(2,1)}, u32[]{:S(2)}, u32[]{:S(2)}) collective-permute-start(bf16[2048,256]{1,0:T(8,128)(2,1)} %get-tuple-element.68), channel_id=1, source_target_pairs={{0,1},{1,2},{2,3},{3,0},{4,5},{5,6},{6,7},{7,4},{8,9},{9,10},{10,1... | collective-permute-start | bytes 3145736 | tf_op jit(solution)/shard_map/ppermute | solution.py:39
  186.6 27.4 %collective-permute-start.4 = (bf16[2048,256]{1,0:T(8,128)(2,1)}, bf16[2048,256]{1,0:T(8,128)(2,1)}, u32[]{:S(2)}, u32[]{:S(2)}) collective-permute-start(bf16[2048,256]{1,0:T(8,128)(2,1)} %get-tuple-element.68), channel_id=1, source_target_pairs={{0,3},{1,0},{2,1},{3,2},{4,7},{5,4},{6,5},{7,6},{8,11},{9,8},{10,9... | collective-permute-start | bytes 3145736 | tf_op jit(solution)/shard_map/ppermute | solution.py:44
  210.4 14.5 %collective-permute-start.5 = (bf16[2048,256]{1,0:T(8,128)(2,1)}, bf16[2048,256]{1,0:T(8,128)(2,1)}, u32[]{:S(2)}, u32[]{:S(2)}) collective-permute-start(bf16[2048,256]{1,0:T(8,128)(2,1)} %collective-permute-done.3), channel_id=1, source_target_pairs={{0,1},{1,2},{2,3},{3,0},{4,5},{5,6},{6,7},{7,4},{8,9},{9,10},{10,1... | collective-permute-start | bytes 3145736 | tf_op jit(solution)/shard_map/ppermute | solution.py:39
  214.0 13.2 %copy-start.44 = (f32[1024]{0:T(1024)S(1)}, f32[1024]{0:T(1024)}, u32[]{:S(2)}) copy-start(f32[1024]{0:T(1024)} %param.37) | copy-start | bytes 12292
  214.0 13.3 %copy-start.51 = (bf16[1024,1024]{1,0:T(8,128)(2,1)S(1)}, bf16[1024,1024]{1,0:T(8,128)(2,1)}, u32[]{:S(2)}) copy-start(bf16[1024,1024]{1,0:T(8,128)(2,1)} %param.36) | copy-start | bytes 6291460
  236.3 1.9 copy-start.56
  244.3 46.1 %copy-start.39 = (f32[256]{0:T(256)S(1)}, f32[256]{0:T(256)}, u32[]{:S(2)}) copy-start(f32[256]{0:T(256)} %param.39) | copy-start | bytes 3076
  244.3 121.7 %all-gather.3.cloned.1.call-start = ((), (), s32[]{:S(2)}) async-start(), calls=%async_computation.6 | async-start | bytes 5242880 | tf_op jit(solution)/shard_map/all_gather | solution.py:109
  292.8 14.4 %copy-start.45 = (f32[256]{0:T(256)S(1)}, f32[256]{0:T(256)}, u32[]{:S(2)}) copy-start(f32[256]{0:T(256)} %param.41) | copy-start | bytes 3076
  292.8 14.4 %copy-start.46 = (f32[256]{0:T(256)S(1)}, f32[256]{0:T(256)}, u32[]{:S(2)}) copy-start(f32[256]{0:T(256)} %param.40) | copy-start | bytes 3076
  330.1 101.2 %reduce-scatter.9.cloned.1.call-start = ((), (), s32[]{:S(2)}) async-start(), calls=%async_computation.7 | async-start | bytes 5242880 | tf_op jit(solution)/shard_map/reduce_scatter | solution.py:113
  366.0 14.3 %copy-start.52 = (bf16[1024,1024]{1,0:T(8,128)(2,1)S(1)}, bf16[1024,1024]{1,0:T(8,128)(2,1)}, u32[]{:S(2)}) copy-start(bf16[1024,1024]{1,0:T(8,128)(2,1)} %param.36) | copy-start | bytes 6291460
  378.4 2.0 copy-start.58
  386.7 44.6 %copy-start.4 = (bf16[2048,256]{1,0:T(8,128)(2,1)S(1)}, bf16[2048,256]{1,0:T(8,128)(2,1)}, u32[]{:S(2)}) copy-start(bf16[2048,256]{1,0:T(8,128)(2,1)} %reduce-scatter.5.cloned.1.call-done) | copy-start | bytes 3145732
  386.7 44.6 %copy-start.9 = (bf16[2048,256]{1,0:T(8,128)(2,1)S(1)}, bf16[2048,256]{1,0:T(8,128)(2,1)}, u32[]{:S(2)}) copy-start(bf16[2048,256]{1,0:T(8,128)(2,1)} %reduce-scatter.7.cloned.1.call-done) | copy-start | bytes 3145732
  386.7 99.9 %all-gather.5.cloned.1.call-start = ((), (), s32[]{:S(2)}) async-start(), calls=%async_computation.8 | async-start | bytes 5242880 | tf_op jit(solution)/shard_map/all_gather | solution.py:109
  448.4 1.3 copy-start.7
  449.7 2.0 copy-start.6
  450.9 314.4 %all-reduce.8.cloned.1.call-start = ((), (), s32[]{:S(2)}) async-start(), calls=%async_computation.10 | async-start | bytes 12582912 | tf_op jit(solution)/shard_map/psum | solution.py:339
  453.5 9.5 %copy-start.50 = (bf16[2048,1024]{1,0:T(8,128)(2,1)S(1)}, bf16[2048,1024]{1,0:T(8,128)(2,1)}, u32[]{:S(2)}) copy-start(bf16[2048,1024]{1,0:T(8,128)(2,1)} %all-gather.3.cloned.1.call-done) | copy-start | bytes 12582916
  453.5 9.5 %copy-start.57 = (bf16[2048,1024]{1,0:T(8,128)(2,1)S(1)}, bf16[2048,1024]{1,0:T(8,128)(2,1)}, u32[]{:S(2)}) copy-start(bf16[2048,1024]{1,0:T(8,128)(2,1)} %copy-done.56) | copy-start | bytes 12582916
  463.0 23.6 %copy-start.25 = (bf16[256,1024]{1,0:T(8,128)(2,1)S(1)}, bf16[256,1024]{1,0:T(8,128)(2,1)}, u32[]{:S(2)}) copy-start(bf16[256,1024]{1,0:T(8,128)(2,1)} %param.32) | copy-start | bytes 1572868
  497.2 4.8 copy-start.41
  502.0 9.3 %copy-start.8 = (f32[4,512,4,64]{1,3,2,0:T(8,128)S(1)}, f32[4,512,4,64]{1,3,2,0:T(8,128)}, u32[]{:S(2)}) copy-start(f32[4,512,4,64]{1,3,2,0:T(8,128)} %copy.110) | copy-start | bytes 6291460
  502.0 9.3 %copy-start.21 = (bf16[4,512,4,64]{1,3,2,0:T(8,128)(2,1)S(1)}, bf16[4,512,4,64]{1,3,2,0:T(8,128)(2,1)}, u32[]{:S(2)}) copy-start(bf16[4,512,4,64]{1,3,2,0:T(8,128)(2,1)} %copy.106) | copy-start | bytes 3145732
  522.7 12.1 %copy-start.10 = (bf16[4,512,4,64]{1,3,2,0:T(8,128)(2,1)S(1)}, bf16[4,512,4,64]{1,3,2,0:T(8,128)(2,1)}, u32[]{:S(2)}) copy-start(bf16[4,512,4,64]{1,3,2,0:T(8,128)(2,1)} %copy.104) | copy-start | bytes 3145732
  534.9 2.6 copy-start.11
  539.1 2.6 copy-start.19
  540.2 3.6 copy-start.15
  548.0 2.2 copy-start.13
  548.1 2.8 copy-start.12
  553.0 1.4 copy-start.26
  553.0 2.6 copy-start.28
  553.0 258.3 %reduce-scatter.11.cloned.1.call-start = ((), (), s32[]{:S(2)}) async-start(), calls=%async_computation.9 | async-start | bytes 5242880 | tf_op jit(solution)/shard_map/reduce_scatter | solution.py:113
  555.6 1.3 copy-start.16
  555.6 1.3 copy-start.29
  560.4 1.3 copy-start.42
  560.4 3.2 copy-start.48
  560.4 4.4 copy-start.33
  560.4 5.7 copy-start.35
  614.2 7.1 copy-start.37
  614.2 7.1 copy-start.43
  614.2 7.5 copy-start.49
  765.3 4.4 copy-start.31
  765.3 5.5 copy-start.30
  767.5 4.4 copy-start.23
  771.9 2.6 copy-start.22
  774.5 40.1 %copy-start.1 = (bf16[1024,1024]{1,0:T(8,128)(2,1)S(1)}, bf16[1024,1024]{1,0:T(8,128)(2,1)}, u32[]{:S(2)}) copy-start(bf16[1024,1024]{1,0:T(8,128)(2,1)} %param.38) | copy-start | bytes 6291460
  (8 other events, 8.3 us)
Sparse Core Ops, SparseCore 0:
  118.2 48.1 reduce-scatter.4
  244.4 45.9 reduce-scatter.6
  330.2 35.7 all-gather.2
  386.9 44.3 reduce-scatter.8
  451.0 35.5 all-gather.4
  553.1 212.1 all-reduce.7
  767.8 43.3 reduce-scatter.10
